TPU v7x, 256 devices: a whole 4x4x8 slice. The times are simulated.
256 devices in a mesh: role: 2 (over core), dev: 64 (over x_hi, y, z), head: 2 (over x_lo).
Axes of the slice: x: 4 (x_hi: 2, x_lo: 2; x = x_hi * 2 + x_lo), y: 4, z: 8, core: 2. Of those that a mesh axis runs over, the one named last changes fastest.
Arguments:
- hidden: bfloat16 [2048, 4096], P(('role', 'dev', 'head')), may hold values from -6 to 6
- queries: bfloat16 [2048, 64, 128], P(('role', 'dev'), 'head'), as said below
- cache_keys: bfloat16 [2048, 128, 4, 128], P(('role', 'dev'), None, 'head'), as said below
- cache_values: bfloat16 [2048, 128, 4, 128], P(('role', 'dev'), None, 'head'), may hold values from -6 to 6
- new_keys: bfloat16 [2048, 4, 128], P(('role', 'dev'), 'head'), may hold values from -6 to 6
- new_values: bfloat16 [2048, 4, 128], P(('role', 'dev'), 'head'), may hold values from -6 to 6
- lengths: int32 [2048], P(('role', 'dev')), may hold values from 32 to 128, as said below
- out_proj: bfloat16 [8192, 4096], P('head', 'dev'), may hold values from -0.5 to 0.5
- norm_gain: float32 [4096], replicated, may hold values from 0.1 to 1.9
- expert_gate: bfloat16 [128, 4096, 768], P(('role', 'dev'), None, 'head'), may hold values from -0.09375 to 0.09375
- expert_up: bfloat16 [128, 4096, 768], P(('role', 'dev'), None, 'head'), may hold values from -0.09375 to 0.09375
- expert_down: bfloat16 [128, 768, 4096], P(('role', 'dev'), 'head'), may hold values from -0.21875 to 0.21875
- expert_ids: int32 [2048, 8], P(('role', 'dev', 'head')), may hold values from 0 to 127, all different within a row; in each aligned block of 8 rows (0 to 7, 8 to 15, ...) at most 2 rows name the same one
- gate_levels: int32 [2048, 8], P(('role', 'dev', 'head')), may hold values from 1 to 255
Outputs:
- layer_out: bfloat16 [2048, 4096], P(('role', 'dev', 'head'))
Inputs may be any that keep to these rules, and one draw needn't show every extreme that they name: `queries`: query vectors of the new tokens. `cache_keys`: cached keys of the requests. `lengths`: the first request of each block of 16 rows holds 128 positions and the second holds 32. `expert_ids`: each row names 8 different experts; among the 8 rows of one device no expert is named more than 2 times, a bound that some block reaches.
All inputs are finite; a program needn't handle non-finite values.
Results may differ from a plain program's by a relative error of at most 0.0065.
Values may be sent and summed in bfloat16 or wider, within the bound.
No kernel may reach another device: no remote copies, remote signals or barrier semaphores. Data moves between devices by JAX's collectives and lax.ppermute only.
A program may use at most 64 MiB of HBM per device.

v0:
```python
import math
import jax
import jax.numpy as jnp
from jax import lax
from jax.sharding import PartitionSpec as P


def attend_block(query_rows, key_rows, value_rows, key_new, value_new, valid_len):
    row_count = query_rows.shape[0]
    kv_heads = key_rows.shape[2]
    group_size = query_rows.shape[1] // kv_heads
    head_dim = query_rows.shape[2]
    scaling = 1.0 / math.sqrt(head_dim)
    query_f = query_rows.astype(jnp.float32).reshape(row_count, kv_heads, group_size, head_dim)
    scores = jnp.einsum("bhgd,bthd->bhgt", query_f, key_rows.astype(jnp.float32)) * scaling
    scores_new = jnp.einsum("bhgd,bhd->bhg", query_f, key_new.astype(jnp.float32)) * scaling
    positions = jnp.arange(key_rows.shape[1], dtype=jnp.int32)
    usable = (positions[None, :] < valid_len[:, None])[:, None, None, :]
    masked = jnp.where(usable, scores, -1e30)
    highest = jnp.maximum(jnp.max(masked, axis=-1), scores_new)
    exp_terms = jnp.exp(masked - highest[..., None])
    exp_new = jnp.exp(scores_new - highest)
    totals = jnp.sum(exp_terms, axis=-1) + exp_new
    weights = (exp_terms / totals[..., None]).astype(jnp.bfloat16)
    weight_new = (exp_new / totals).astype(jnp.bfloat16)
    blended = jnp.einsum("bhgt,bthd->bhgd", weights, value_rows, preferred_element_type=jnp.float32)
    blended = (
        blended
        + weight_new.astype(jnp.float32)[..., None] * value_new.astype(jnp.float32)[:, :, None, :]
    )
    return blended.astype(jnp.bfloat16).reshape(row_count, kv_heads * group_size * head_dim)


def expert_rows(rows_in, gate_w, up_w, down_w):
    gate_part = jnp.dot(rows_in, gate_w, preferred_element_type=jnp.float32)
    up_part = jnp.dot(rows_in, up_w, preferred_element_type=jnp.float32)
    active = (jax.nn.silu(gate_part) * up_part).astype(jnp.bfloat16)
    return jnp.dot(active, down_w, preferred_element_type=jnp.float32)


def slot_ranks(flat_ids, experts):
    one_hot = (flat_ids[:, None] == jnp.arange(experts, dtype=jnp.int32)[None, :]).astype(jnp.int32)
    return jnp.sum(jnp.cumsum(one_hot, axis=0) * one_hot, axis=1) - 1


def on_device(
    hidden,
    queries,
    cache_keys,
    cache_values,
    new_keys,
    new_values,
    lengths,
    out_proj,
    norm_gain,
    expert_gate,
    expert_up,
    expert_down,
    expert_ids,
    gate_levels,
):
    attended = attend_block(queries, cache_keys, cache_values, new_keys, new_values, lengths)
    columns = jnp.dot(
        lax.all_gather(attended, "dev", axis=0, tiled=True),
        out_proj,
        preferred_element_type=jnp.float32,
    )
    dev_count = lax.axis_size("dev")
    head_count = lax.axis_size("head")
    experts = lax.axis_size("role") * dev_count
    col_width = out_proj.shape[1]
    width = dev_count * col_width
    projected = lax.all_to_all(columns, ("dev", "head"), split_axis=0, concat_axis=1, tiled=True)
    tokens = projected.shape[0]
    summed = jnp.sum(projected.reshape(tokens, dev_count, head_count, col_width), axis=2).reshape(
        tokens, width
    )
    residual = hidden.astype(jnp.float32) + summed
    normed = (
        residual
        * lax.rsqrt(jnp.mean(residual * residual, axis=-1, keepdims=True) + 1e-06)
        * norm_gain
    ).astype(jnp.bfloat16)
    top_k = expert_ids.shape[1]
    capacity = max(2, 2 * tokens * top_k // experts)
    own_ids = expert_ids.reshape(-1)
    own_ranks = slot_ranks(own_ids, experts)
    pair_rows, pair_ids = (
        lax.all_gather(normed, "head", axis=0, tiled=True),
        lax.all_gather(expert_ids, "head", axis=0, tiled=True),
    )
    pair_flat = pair_ids.reshape(head_count, tokens * top_k)
    pair_ranks = jax.vmap(lambda id_row: slot_ranks(id_row, experts))(pair_flat)
    pair_ranks = pair_ranks + capacity * jnp.arange(head_count, dtype=jnp.int32)[:, None]
    rows_from = jnp.arange(head_count * tokens * top_k, dtype=jnp.int32) // top_k
    outgoing = (
        jnp.zeros((experts, head_count * capacity, width), jnp.bfloat16)
        .at[pair_flat.reshape(-1), pair_ranks.reshape(-1)]
        .set(pair_rows[rows_from])
    )
    incoming = lax.all_to_all(outgoing, ("role", "dev"), split_axis=0, concat_axis=0, tiled=True)
    sources = incoming.shape[0]
    slot_total = incoming.shape[1]
    partial_value = expert_rows(
        incoming.reshape(sources * slot_total, width), expert_gate[0], expert_up[0], expert_down[0]
    )
    partial_value = partial_value.reshape(sources, slot_total, width).astype(jnp.bfloat16)
    arrived = lax.all_to_all(
        partial_value, ("role", "dev"), split_axis=0, concat_axis=0, tiled=True
    )
    arrived = (
        lax.psum_scatter(arrived, "head", scatter_dimension=1, tiled=True)
        .astype(jnp.float32)
        .astype(jnp.bfloat16)
    )
    picked = arrived[own_ids, own_ranks].astype(jnp.float32).reshape(tokens, top_k, width)
    levels = gate_levels.astype(jnp.float32)
    shares = levels / jnp.sum(levels, axis=1, keepdims=True)
    return (residual + jnp.sum(shares[..., None] * picked, axis=1)).astype(jnp.bfloat16)


def solution(mesh):
    placed = (
        P(("role", "dev", "head"), None),
        P(("role", "dev"), "head", None),
        P(("role", "dev"), None, "head", None),
        P(("role", "dev"), None, "head", None),
        P(("role", "dev"), "head", None),
        P(("role", "dev"), "head", None),
        P(("role", "dev")),
        P("head", "dev"),
        P(),
        P(("role", "dev"), None, "head"),
        P(("role", "dev"), None, "head"),
        P(("role", "dev"), "head", None),
        P(("role", "dev", "head"), None),
        P(("role", "dev", "head"), None),
    )
    return jax.shard_map(
        on_device,
        mesh=mesh,
        in_specs=placed,
        out_specs=P(("role", "dev", "head"), None),
        check_vma=False,
    )
```

profile of v0, /device:TPU:1, one launch (start us, length us, event | category | flops | bytes accessed | tf_op | source)
XLA Modules:
  0.0 560.9 jit_solution(16563779175409254275)
XLA Ops:
  8.6 2.1 fusion.34
  14.1 3.7 all_gather.10
  18.3 148.0 %all-gather.2.cloned.1.call-done = bf16[1024,4096]{1,0:T(8,128)(2,1)} async-done(((bf16[16,4096]{1,0:T(8,128)(2,1)}), bf16[1024,4096]{1,0:T(8,128)(2,1)}) %all-gather.2.cloned.1.call-update) | async-done | bytes 8388624 | tf_op jit(solution)/shard_map/all_gather | solution.py:64
  166.3 6.6 %convolution_bitcast_fusion = f32[128,8,64]{2,1,0:T(8,128)} fusion(bf16[1024,4096]{1,0:T(8,128)(2,1)} %all-gather.2.cloned.1.call-done, bf16[4096,64]{0,1:T(8,128)(2,1)} %param.21), kind=kOutput, calls=%fused_computation.11 | convolution fusion | flops 536870912 | bytes 9175040 | tf_op jit(solution)/shard_map/dot_general | solution.py:63
  172.9 2.1 reshape.251
  175.0 9.4 %all-to-all-start = ((f32[128,1,512]{2,1,0:T(1,128)}), f32[128,1,512]{2,1,0:T(1,128)S(1)}, u32[]{:S(2)}, u32[]{:S(2)}) async-start(f32[128,1,512]{2,1,0:T(1,128)} %reshape.251), calls=%async_computation | async-start | bytes 524288 | tf_op jit(solution)/shard_map/all_to_all | solution.py:73
  184.8 11.2 %all-to-all-done = f32[128,1,512]{2,1,0:T(1,128)S(1)} async-done(((f32[128,1,512]{2,1,0:T(1,128)}), f32[128,1,512]{2,1,0:T(1,128)S(1)}, u32[]{:S(2)}, u32[]{:S(2)}) %all-to-all-start) | async-done | bytes 262176 | tf_op jit(solution)/shard_map/all_to_all | solution.py:73
  197.2 2.2 reduce
  203.6 3.8 all_gather.11
  207.4 2.2 gather_fusion
  209.5 4.0 broadcast_in_dim.16
  213.6 32.4 %scatter_fusion = bf16[128,4,4096]{2,1,0:T(4,128)(2,1)} fusion(bf16[128,4,4096]{2,1,0:T(4,128)(2,1)} %broadcast_in_dim.16, s32[128]{0:T(128)S(1)} %fusion.32, bf16[128,4096]{1,0:T(8,128)(2,1)} %gather_fusion), kind=kCustom, calls=%fused_computation.2 | custom fusion | bytes 3146752 | tf_op jit(solution)/shard_map/scatter | solution.py:99
  246.0 112.3 %all_to_all.26 = bf16[128,4,4096]{2,1,0:T(4,128)(2,1)} all-to-all(bf16[128,4,4096]{2,1,0:T(4,128)(2,1)} %scatter_fusion), channel_id=1, replica_groups=mesh['role'=2,'dev'=64,'head'=2] {'role','dev'}, dimensions={0} | all-to-all | bytes 8388608 | tf_op jit(solution)/shard_map/all_to_all | solution.py:101
  358.3 6.9 %reshape.225 = bf16[512,4096]{1,0:T(8,128)(2,1)} reshape(bf16[128,4,4096]{2,1,0:T(4,128)(2,1)} %all_to_all.26) | data formatting | bytes 8388608 | tf_op jit(solution)/shard_map/reshape | solution.py:105
  365.2 5.6 %fusion.3 = f32[512,384]{1,0:T(8,128)S(1)} fusion(bf16[512,4096]{1,0:T(8,128)(2,1)} %reshape.225, bf16[1,4096,384]{2,1,0:T(8,128)(2,1)} %param.23), kind=kOutput, calls=%fused_computation.7 | convolution fusion | flops 1610612736 | bytes 8126464 | tf_op jit(solution)/shard_map/dot_general | solution.py:35
  370.8 3.1 fusion.8
  373.9 1.8 dot_general.29
  375.8 3.3 convolution_convert_fusion
  379.1 3.2 copy.35
  382.3 104.9 %all_to_all.27 = bf16[128,4,4096]{2,1,0:T(4,128)(2,1)S(1)} all-to-all(bf16[128,4,4096]{2,1,0:T(4,128)(2,1)S(1)} %copy.35), channel_id=1, replica_groups=mesh['role'=2,'dev'=64,'head'=2] {'role','dev'}, dimensions={0} | all-to-all | bytes 8388608 | tf_op jit(solution)/shard_map/all_to_all | solution.py:108
  487.3 4.2 copy.36
  492.6 50.9 %reduce-scatter.2.cloned.1.call-done = bf16[128,2,4096]{2,0,1:T(8,128)(2,1)} async-done(((bf16[128,4,4096]{2,0,1:T(8,128)(2,1)}), bf16[128,2,4096]{2,0,1:T(8,128)(2,1)}) %reduce-scatter.2.cloned.1.call-update) | async-done | bytes 2097168 | tf_op jit(solution)/shard_map/reduce_scatter | solution.py:112
  543.5 5.1 copy.37
  548.6 3.3 gather_fusion.1
  (57 shorter events, 14.8 us)
Async XLA Ops:
  6.5 369.2 %copy-start = (bf16[1,384,4096]{2,1,0:T(8,128)(2,1)S(1)}, bf16[1,384,4096]{2,1,0:T(8,128)(2,1)}, u32[]{:S(2)}) copy-start(bf16[1,384,4096]{2,1,0:T(8,128)(2,1)} %param.25) | copy-start | bytes 9437188
  6.5 7.6 %copy-start.4 = (s32[8,8]{1,0:T(8,128)S(1)}, s32[8,8]{1,0:T(8,128)}, u32[]{:S(2)}) copy-start(s32[8,8]{1,0:T(8,128)} %param.26) | copy-start | bytes 772
  6.5 159.8 %all-gather.2.cloned.1.call-start = ((), (), s32[]{:S(2)}) async-start(), calls=%async_computation.4 | async-start | bytes 8519680 | tf_op jit(solution)/shard_map/all_gather | solution.py:64
  172.9 30.4 %copy-start.3 = (bf16[8,4096]{1,0:T(8,128)(2,1)S(1)}, bf16[8,4096]{1,0:T(8,128)(2,1)}, u32[]{:S(2)}) copy-start(bf16[8,4096]{1,0:T(8,128)(2,1)} %param.14) | copy-start | bytes 196612
  172.9 30.6 %copy-start.5 = (f32[4096]{0:T(1024)S(1)}, f32[4096]{0:T(1024)}, u32[]{:S(2)}) copy-start(f32[4096]{0:T(1024)} %param.22) | copy-start | bytes 49156
  175.0 21.0 %all-to-all-start = ((f32[128,1,512]{2,1,0:T(1,128)}), f32[128,1,512]{2,1,0:T(1,128)S(1)}, u32[]{:S(2)}, u32[]{:S(2)}) async-start(f32[128,1,512]{2,1,0:T(1,128)} %reshape.251), calls=%async_computation | async-start | bytes 524288 | tf_op jit(solution)/shard_map/all_to_all | solution.py:73
  184.5 359.0 %reduce-scatter.2.cloned.1.call-start = ((), (), s32[]{:S(2)}) async-start(), calls=%async_computation.5 | async-start | bytes 6291456 | tf_op jit(solution)/shard_map/reduce_scatter | solution.py:112
  196.0 0.7 copy-start.2
  365.2 5.6 %copy-start.1 = (bf16[512,4096]{1,0:T(8,128)(2,1)S(1)}, bf16[512,4096]{1,0:T(8,128)(2,1)}, u32[]{:S(2)}) copy-start(bf16[512,4096]{1,0:T(8,128)(2,1)} %reshape.225) | copy-start | bytes 12582916
  365.2 5.6 %copy-start.7 = (bf16[1,4096,384]{2,1,0:T(8,128)(2,1)S(1)}, bf16[1,4096,384]{2,1,0:T(8,128)(2,1)}, u32[]{:S(2)}) copy-start(bf16[1,4096,384]{2,1,0:T(8,128)(2,1)} %param.24) | copy-start | bytes 9437188
  491.5 0.7 copy-start.6
Sparse Core Ops, SparseCore 0:
  14.3 152.0 all-gather.1
  491.6 51.7 reduce-scatter.1
where the time goes:
time: 562 us; the launch traced here: 561 us
  blocking collectives  225 us (40%)
  waiting for transfers between devices  210 us (37%)
  local copies, waits for them, and re-layouts  70.8 us (13%)
  matrix products  23.5 us (4%)
  between operations  13.6 us (2%)
  starting transfers between devices  9.48 us (2%)
  other arithmetic  8.69 us (2%)
    all_gather x1, waiting for transfers between devices, on_device(): lax.all_gather(attended, 'dev', axis=0, tiled=True)  148 us
    all_to_all x1, blocking collectives, on_device(): lax.all_to_all(outgoing, ('role', 'dev'), split_axis=0, concat_axis=0, ti...  112 us
    all_to_all x1, blocking collectives, on_device(): lax.all_to_all(partial_value, ('role', 'dev'), split_axis=0, concat_axis=...  105 us
    reduce_scatter x1, waiting for transfers between devices, on_device(): lax.psum_scatter(arrived, 'head', scatter_dimension=1, tiled=True)  50.9 us
    scatter x1, local copies, waits for them, and re-layouts, on_device(): outgoing = jnp.zeros((experts, head_count * capacity, width), jnp.bfloat1...  32.4 us
  transfers between devices with their start and end apart: 3, of which 3 were waited for; matrix products, arithmetic and copies ran while one was open for 0% of the time, Pallas kernels for 0%

commit v1 on v0

--- a/solution.py
+++ b/solution.py
@@ -70,7 +70,15 @@
     experts = lax.axis_size("role") * dev_count
     col_width = out_proj.shape[1]
     width = dev_count * col_width
-    projected = lax.all_to_all(columns, ("dev", "head"), split_axis=0, concat_axis=1, tiled=True)
+    projected = jnp.concatenate(
+        lax.all_to_all(
+            jnp.stack(jnp.split(columns, lax.axis_size(("dev", "head")), axis=0)),
+            ("dev", "head"),
+            0,
+            0,
+        ),
+        axis=1,
+    )
     tokens = projected.shape[0]
     summed = jnp.sum(projected.reshape(tokens, dev_count, head_count, col_width), axis=2).reshape(
         tokens, width

time: 562 us -> 657 us (1.17)
  local copies, waits for them, and re-layouts: 70.8 us -> 164 us
    unnamed x19 -> x145, local copies, waits for them, and re-layouts: 4.77 us -> 93.6 us
where the time goes in v1:
time: 657 us; the launch traced here: 655 us
  blocking collectives  225 us (34%)
  waiting for transfers between devices  210 us (32%)
  local copies, waits for them, and re-layouts  164 us (25%)
  matrix products  23 us (4%)
  between operations  13.6 us (2%)
  other arithmetic  10.1 us (2%)
  starting transfers between devices  10 us (2%)
    all_gather x1, waiting for transfers between devices, on_device(): lax.all_gather(attended, 'dev', axis=0, tiled=True)  148 us
    all_to_all x1, blocking collectives, on_device(): lax.all_to_all(outgoing, ('role', 'dev'), split_axis=0, concat_axis=0, ti...  112 us
    all_to_all x1, blocking collectives, on_device(): lax.all_to_all(partial_value, ('role', 'dev'), split_axis=0, concat_axis=...  105 us
    unnamed x145, local copies, waits for them, and re-layouts  93.6 us
    reduce_scatter x1, waiting for transfers between devices, on_device(): lax.psum_scatter(arrived, 'head', scatter_dimension=1, tiled=True)  50.9 us
    scatter x1, local copies, waits for them, and re-layouts, on_device(): outgoing = jnp.zeros((experts, head_count * capacity, width), jnp.bfloat1...  32.4 us
  transfers between devices with their start and end apart: 3, of which 3 were waited for; matrix products, arithmetic and copies ran while one was open for 0% of the time, Pallas kernels for 0%

profile of v1, /device:TPU:1, one launch (start us, length us, event | category | flops | bytes accessed | tf_op | source)
XLA Modules:
  0.0 655.3 jit_solution(2162875574379702101)
XLA Ops:
  14.1 3.7 all_gather.10
  18.3 148.0 %all-gather.2.cloned.1.call-done = bf16[1024,4096]{1,0:T(8,128)(2,1)} async-done(((bf16[16,4096]{1,0:T(8,128)(2,1)}), bf16[1024,4096]{1,0:T(8,128)(2,1)}) %all-gather.2.cloned.1.call-update) | async-done | bytes 8388624 | tf_op jit(solution)/shard_map/all_gather | solution.py:64
  166.3 6.1 fusion.35
  258.8 3.5 copy.297
  264.4 10.0 %all-to-all-start = ((f32[128,1,512]{2,1,0:T(1,128)}), f32[128,1,512]{2,1,0:T(1,128)}, u32[]{:S(2)}, u32[]{:S(2)}) async-start(f32[128,1,512]{2,1,0:T(1,128)} %reshape.247), calls=%async_computation | async-start | bytes 524288 | tf_op jit(solution)/shard_map/all_to_all | solution.py:74
  274.7 10.8 %all-to-all-done = f32[128,1,512]{2,1,0:T(1,128)} async-done(((f32[128,1,512]{2,1,0:T(1,128)}), f32[128,1,512]{2,1,0:T(1,128)}, u32[]{:S(2)}, u32[]{:S(2)}) %all-to-all-start) | async-done | bytes 262176 | tf_op jit(solution)/shard_map/all_to_all | solution.py:74
  286.0 2.9 reduce
  292.6 2.9 copy.307
  295.6 2.2 copy.306
  298.0 4.0 all_gather.11
  302.0 2.2 gather_fusion
  304.1 4.0 broadcast_in_dim.16
  308.1 32.4 %scatter_fusion = bf16[128,4,4096]{2,1,0:T(4,128)(2,1)} fusion(bf16[128,4,4096]{2,1,0:T(4,128)(2,1)} %broadcast_in_dim.16, s32[128]{0:T(128)S(1)} %fusion.32, bf16[128,4096]{1,0:T(8,128)(2,1)} %gather_fusion), kind=kCustom, calls=%fused_computation.2 | custom fusion | bytes 3146752 | tf_op jit(solution)/shard_map/scatter | solution.py:107
  340.6 112.1 %all_to_all.15 = bf16[128,4,4096]{2,1,0:T(4,128)(2,1)} all-to-all(bf16[128,4,4096]{2,1,0:T(4,128)(2,1)} %scatter_fusion), channel_id=1, replica_groups=mesh['role'=2,'dev'=64,'head'=2] {'role','dev'}, dimensions={0} | all-to-all | bytes 8388608 | tf_op jit(solution)/shard_map/all_to_all | solution.py:109
  452.7 6.9 %reshape.221 = bf16[512,4096]{1,0:T(8,128)(2,1)} reshape(bf16[128,4,4096]{2,1,0:T(4,128)(2,1)} %all_to_all.15) | data formatting | bytes 8388608 | tf_op jit(solution)/shard_map/reshape | solution.py:113
  459.6 5.6 fusion.3
  465.2 3.1 fusion.8
  470.2 3.3 convolution_convert_fusion
  473.5 3.2 copy.301
  476.8 104.9 %all_to_all.16 = bf16[128,4,4096]{2,1,0:T(4,128)(2,1)S(1)} all-to-all(bf16[128,4,4096]{2,1,0:T(4,128)(2,1)S(1)} %copy.301), channel_id=1, replica_groups=mesh['role'=2,'dev'=64,'head'=2] {'role','dev'}, dimensions={0} | all-to-all | bytes 8388608 | tf_op jit(solution)/shard_map/all_to_all | solution.py:116
  581.7 4.2 copy.302
  587.0 50.9 %reduce-scatter.2.cloned.1.call-done = bf16[128,2,4096]{2,0,1:T(8,128)(2,1)} async-done(((bf16[128,4,4096]{2,0,1:T(8,128)(2,1)}), bf16[128,2,4096]{2,0,1:T(8,128)(2,1)}) %reduce-scatter.2.cloned.1.call-update) | async-done | bytes 2097168 | tf_op jit(solution)/shard_map/reduce_scatter | solution.py:120
  637.9 5.1 copy.303
  643.0 3.3 gather_fusion.1
  (184 shorter events, 106.2 us)
Async XLA Ops:
  6.5 463.6 %copy-start = (bf16[1,384,4096]{2,1,0:T(8,128)(2,1)S(1)}, bf16[1,384,4096]{2,1,0:T(8,128)(2,1)}, u32[]{:S(2)}) copy-start(bf16[1,384,4096]{2,1,0:T(8,128)(2,1)} %param.25) | copy-start | bytes 9437188
  6.5 7.6 %copy-start.3 = (s32[8,8]{1,0:T(8,128)S(1)}, s32[8,8]{1,0:T(8,128)}, u32[]{:S(2)}) copy-start(s32[8,8]{1,0:T(8,128)} %param.26) | copy-start | bytes 772
  6.5 159.8 %all-gather.2.cloned.1.call-start = ((), (), s32[]{:S(2)}) async-start(), calls=%async_computation.4 | async-start | bytes 8519680 | tf_op jit(solution)/shard_map/all_gather | solution.py:64
  262.3 35.4 %copy-start.2 = (bf16[8,4096]{1,0:T(8,128)(2,1)S(1)}, bf16[8,4096]{1,0:T(8,128)(2,1)}, u32[]{:S(2)}) copy-start(bf16[8,4096]{1,0:T(8,128)(2,1)} %param.14) | copy-start | bytes 196612
  262.3 35.6 %copy-start.4 = (f32[4096]{0:T(1024)S(1)}, f32[4096]{0:T(1024)}, u32[]{:S(2)}) copy-start(f32[4096]{0:T(1024)} %param.22) | copy-start | bytes 49156
  264.4 21.1 %all-to-all-start = ((f32[128,1,512]{2,1,0:T(1,128)}), f32[128,1,512]{2,1,0:T(1,128)}, u32[]{:S(2)}, u32[]{:S(2)}) async-start(f32[128,1,512]{2,1,0:T(1,128)} %reshape.247), calls=%async_computation | async-start | bytes 524288 | tf_op jit(solution)/shard_map/all_to_all | solution.py:74
  274.4 363.5 %reduce-scatter.2.cloned.1.call-start = ((), (), s32[]{:S(2)}) async-start(), calls=%async_computation.5 | async-start | bytes 6291456 | tf_op jit(solution)/shard_map/reduce_scatter | solution.py:120
  459.6 5.6 copy-start.1
  459.6 5.6 copy-start.6
  585.9 0.7 copy-start.5
Sparse Core Ops, SparseCore 0:
  14.3 152.0 all-gather.1
  586.1 51.7 reduce-scatter.1
